TPU v7x, 32 devices: a whole 2x2x4 slice. The times are simulated.
32 devices in a mesh: ctx: 2 (over x), dp: 4 (over z), tp: 4 (over y, core).
Axes of the slice: x: 2, y: 2, z: 4, core: 2. Of those that a mesh axis runs over, the one named last changes fastest.
Arguments:
- query_act: bfloat16 [4, 4096, 256], P('dp', 'tp', 'ctx'), may hold values from -6 to 6
- key_act: bfloat16 [4, 4096, 256], P('dp', 'tp', 'ctx'), may hold values from -6 to 6
- value_act: bfloat16 [4, 4096, 256], P('dp', 'tp', 'ctx'), may hold values from -6 to 6
- out_grad: bfloat16 [4, 4096, 256], P('dp', 'tp', 'ctx'), may hold values from -6 to 6
- keep_mask: int32 [4, 256], P('dp', 'ctx'), may hold values 0 or 1
- filter_taps: float32 [256, 128], P('tp'), may hold values from -0.5 to 0.5
- skip_gain: float32 [4096], P('tp'), may hold values from -4 to 4
Outputs:
- operator_out: bfloat16 [4, 4096, 256], P('dp', 'tp', 'ctx')
- query_grad: bfloat16 [4, 4096, 256], P('dp', 'tp', 'ctx')
- key_grad: bfloat16 [4, 4096, 256], P('dp', 'tp', 'ctx')
- value_grad: bfloat16 [4, 4096, 256], P('dp', 'tp', 'ctx')
- filter_grad: float32 [256, 128], P('tp')
- skip_grad: float32 [4096], P('tp')
All inputs are finite; a program needn't handle non-finite values. No bound on the sum of `keep_mask` on one device may be relied on, other than what follows from the above.
Results may differ from a plain program's by a relative error of at most 0.007.
Values may be sent and summed in bfloat16 or wider, within the bound.
No kernel may reach another device: no remote copies, remote signals or barrier semaphores. Data moves between devices by JAX's collectives and lax.ppermute only.
A program may use at most 64 MiB of HBM per device.

v0:
```python
import math
import jax
import jax.numpy as jnp
from jax import lax
from jax.sharding import PartitionSpec as P


def tap_matrices(tap_rows):
    tap_len = tap_rows.shape[1]
    source = jnp.arange(tap_len)[:, None]
    target = jnp.arange(tap_len)[None, :]
    spread = tap_rows[:, jnp.mod(target - source, tap_len)]
    nothing = jnp.zeros((), jnp.bfloat16)
    lower_part = jnp.where(target >= source, spread, nothing)
    upper_part = jnp.where(target < source, spread, nothing)
    forward = jnp.concatenate([upper_part, lower_part], axis=1)
    backward = jnp.concatenate(
        [jnp.swapaxes(lower_part, 1, 2), jnp.swapaxes(upper_part, 1, 2)], axis=1
    )
    return (forward, backward)


def diagonal_sums(gram_sums):
    groups, tap_len, double_len = gram_sums.shape
    flattened = gram_sums.reshape(groups, tap_len * double_len)
    flattened = jnp.pad(flattened, ((0, 0), (0, tap_len)))
    skewed = flattened.reshape(groups, tap_len, double_len + 1)
    columns = jnp.sum(skewed, axis=1)
    return columns[:, tap_len:0:-1]


def core(
    query_act, key_act, value_act, scaled_grad, filter_taps, skip_gain, fetch_left, fetch_right
):
    windows, channels, length = query_act.shape
    groups, tap_len = filter_taps.shape
    per_group = channels // groups
    blocks = length // tap_len
    forward, backward = tap_matrices(filter_taps.astype(jnp.bfloat16))
    joined = (key_act.astype(jnp.float32) * value_act.astype(jnp.float32)).astype(jnp.bfloat16)
    before = fetch_left(joined[:, :, length - tap_len :])
    joined_blocks = joined.reshape(windows, channels, blocks, tap_len)
    earlier = jnp.concatenate([before[:, :, None, :], joined_blocks[:, :, :-1, :]], axis=2)
    paired = jnp.concatenate([earlier, joined_blocks], axis=3).reshape(
        windows, groups, per_group, blocks, 2 * tap_len
    )
    mixed_sum = jnp.einsum("wgcbs,gst->wgcbt", paired, forward, preferred_element_type=jnp.float32)
    mixed_sum = mixed_sum.reshape(windows, channels, length) + skip_gain[
        None, :, None
    ] * joined.astype(jnp.float32)
    operator_out = (query_act.astype(jnp.float32) * mixed_sum).astype(jnp.bfloat16)
    mixed_grad = (scaled_grad.astype(jnp.float32) * query_act.astype(jnp.float32)).astype(
        jnp.bfloat16
    )
    query_grad = (scaled_grad.astype(jnp.float32) * mixed_sum).astype(jnp.bfloat16)
    following = fetch_right(mixed_grad[:, :, :tap_len])
    grad_blocks = mixed_grad.reshape(windows, channels, blocks, tap_len)
    next_blocks = jnp.concatenate([grad_blocks[:, :, 1:, :], following[:, :, None, :]], axis=2)
    paired_grad = jnp.concatenate([grad_blocks, next_blocks], axis=3).reshape(
        windows, groups, per_group, blocks, 2 * tap_len
    )
    joined_grad = jnp.einsum(
        "wgcbs,gst->wgcbt", paired_grad, backward, preferred_element_type=jnp.float32
    )
    joined_grad = joined_grad.reshape(windows, channels, length) + skip_gain[
        None, :, None
    ] * mixed_grad.astype(jnp.float32)
    key_grad = (joined_grad * value_act.astype(jnp.float32)).astype(jnp.bfloat16)
    value_grad = (joined_grad * key_act.astype(jnp.float32)).astype(jnp.bfloat16)
    grad_groups = grad_blocks.reshape(windows, groups, per_group, blocks, tap_len)
    gram_sums = jnp.einsum(
        "wgcbt,wgcbs->gts", grad_groups, paired, preferred_element_type=jnp.float32
    )
    tap_sums = diagonal_sums(gram_sums)
    skip_sums = jnp.sum(mixed_grad.astype(jnp.float32) * joined.astype(jnp.float32), axis=(0, 2))
    return (operator_out, query_grad, key_grad, value_grad, tap_sums, skip_sums)


def no_rim(border):
    return jnp.zeros_like(border)


def body(query_act, key_act, value_act, out_grad, keep_mask, filter_taps, skip_gain):
    total_windows = keep_mask.shape[0] * lax.axis_size("dp")
    total_length = query_act.shape[2] * lax.axis_size("ctx")
    per_group = query_act.shape[1] // filter_taps.shape[0]
    tap_scale = 1.0 / math.sqrt(total_windows * total_length * per_group)
    skip_scale = 1.0 / math.sqrt(total_windows * total_length)
    scaled_grad = out_grad * keep_mask.astype(jnp.bfloat16)[:, None, :]
    moved = (
        lax.all_to_all(query_act, "ctx", split_axis=1, concat_axis=2, tiled=True),
        lax.all_to_all(key_act, "ctx", split_axis=1, concat_axis=2, tiled=True),
        lax.all_to_all(value_act, "ctx", split_axis=1, concat_axis=2, tiled=True),
        lax.all_to_all(scaled_grad, "ctx", split_axis=1, concat_axis=2, tiled=True),
    )
    shards = lax.axis_size("ctx")
    position = lax.axis_index("ctx")
    group_count = filter_taps.shape[0] // shards
    own_taps = lax.dynamic_slice_in_dim(filter_taps, position * group_count, group_count, 0)
    own_skip = lax.dynamic_slice_in_dim(
        skip_gain, position * group_count * per_group, group_count * per_group, 0
    )
    results = core(moved[0], moved[1], moved[2], moved[3], own_taps, own_skip, no_rim, no_rim)
    returned = (
        lax.all_to_all(results[0], "ctx", split_axis=2, concat_axis=1, tiled=True),
        lax.all_to_all(results[1], "ctx", split_axis=2, concat_axis=1, tiled=True),
        lax.all_to_all(results[2], "ctx", split_axis=2, concat_axis=1, tiled=True),
        lax.all_to_all(results[3], "ctx", split_axis=2, concat_axis=1, tiled=True),
    )
    replica = lax.psum((results[4], results[5]), "dp")
    gathered = (
        lax.all_gather(replica[0], "ctx", axis=0, tiled=True),
        lax.all_gather(replica[1], "ctx", axis=0, tiled=True),
    )
    tap_sums = gathered[0]
    skip_sums = gathered[1]
    return (
        returned[0],
        returned[1],
        returned[2],
        returned[3],
        tap_sums * tap_scale,
        skip_sums * skip_scale,
    )


def solution(mesh):
    return jax.shard_map(
        body,
        mesh=mesh,
        in_specs=(
            P("dp", "tp", "ctx"),
            P("dp", "tp", "ctx"),
            P("dp", "tp", "ctx"),
            P("dp", "tp", "ctx"),
            P("dp", "ctx"),
            P("tp", None),
            P("tp"),
        ),
        out_specs=(
            P("dp", "tp", "ctx"),
            P("dp", "tp", "ctx"),
            P("dp", "tp", "ctx"),
            P("dp", "tp", "ctx"),
            P("tp", None),
            P("tp"),
        ),
        check_vma=False,
    )
```

profile of v0, /device:TPU:0, one launch (start us, length us, event | category | flops | bytes accessed | tf_op | source)
XLA Modules:
  0.0 214.4 jit_solution(10341014407572912905)
XLA Ops:
  1.3 1.5 fusion.30
  3.3 2.2 %reduce.3 = bf16[1024,128]{1,0:T(8,128)(2,1)S(1)} reduce(bf16[1024,1,128]{2,1,0:T(2,128)(2,1)S(1)} %fusion.30, bf16[]{:T(256)} %broadcast.146), dimensions={1}, to_apply=%fusion.30.reduce_sub_computation | reduce | bytes 524290
  6.3 4.2 %all-to-all-start.4 = ((bf16[2,2,32768]{2,1,0:T(2,128)(2,1)}), bf16[2,2,32768]{2,1,0:T(2,128)(2,1)S(1)}, u32[]{:S(2)}, u32[]{:S(2)}) async-start(bf16[2,2,32768]{2,1,0:T(2,128)(2,1)} %reshape.430), calls=%async_computation.4 | async-start | bytes 524288 | tf_op jit(solution)/shard_map/all_to_all | solution.py:94
  10.8 57.4 %gather_fusion = bf16[16384,32]{1,0:T(8,128)(2,1)} fusion(bf16[32,128]{0,1:T(8,128)(2,1)S(1)} %copy.92, s32[16384]{0:T(1024)S(1)} %fusion.22), kind=kCustom, calls=%fused_computation | custom fusion | bytes 2162688 | tf_op jit(solution)/shard_map/gather | solution.py:12
  68.2 4.0 %copy.82 = bf16[128,128,32]{1,0,2:T(8,128)(2,1)S(1)} copy(bf16[128,128,32]{2,1,0:T(8,128)(2,1)} %bitcast.156) | data formatting | bytes 2097152 | tf_op jit(solution)/shard_map/gather | solution.py:12
  72.2 1.5 bitcast_select_fusion.1
  73.7 1.4 select_bitcast_fusion.1
  75.5 2.2 %reduce.2 = bf16[1024,128]{1,0:T(8,128)(2,1)S(1)} reduce(bf16[1024,1,128]{2,1,0:T(2,128)(2,1)S(1)} %bitcast.187, bf16[]{:T(256)} %broadcast.146), dimensions={1}, to_apply=%bitcast.153.reduce_sub_computation | reduce | bytes 524290
  78.9 2.2 %reduce.4 = bf16[1024,128]{1,0:T(8,128)(2,1)S(1)} reduce(bf16[1024,1,128]{2,1,0:T(2,128)(2,1)S(1)} %bitcast.188, bf16[]{:T(256)} %broadcast.146), dimensions={1}, to_apply=%bitcast.152.reduce_sub_computation | reduce | bytes 524290
  82.3 2.2 %reduce.1 = bf16[1024,128]{1,0:T(8,128)(2,1)S(1)} reduce(bf16[1024,1,128]{2,1,0:T(2,128)(2,1)S(1)} %bitcast.189, bf16[]{:T(256)} %broadcast.146), dimensions={1}, to_apply=%bitcast.151.reduce_sub_computation | reduce | bytes 524290
  85.4 3.5 %all-to-all-start = ((bf16[2,2,32768]{2,1,0:T(2,128)(2,1)}), bf16[2,2,32768]{2,1,0:T(2,128)(2,1)S(1)}, u32[]{:S(2)}, u32[]{:S(2)}) async-start(bf16[2,2,32768]{2,1,0:T(2,128)(2,1)} %reshape.422), calls=%async_computation | async-start | bytes 524288 | tf_op jit(solution)/shard_map/all_to_all | solution.py:91
  89.2 5.5 %all-to-all-done = bf16[2,2,32768]{2,1,0:T(2,128)(2,1)S(1)} async-done(((bf16[2,2,32768]{2,1,0:T(2,128)(2,1)}), bf16[2,2,32768]{2,1,0:T(2,128)(2,1)S(1)}, u32[]{:S(2)}, u32[]{:S(2)}) %all-to-all-start) | async-done | bytes 262176 | tf_op jit(solution)/shard_map/all_to_all | solution.py:91
  94.7 3.4 %all-to-all-start.1 = ((bf16[2,2,32768]{2,1,0:T(2,128)(2,1)}), bf16[2,2,32768]{2,1,0:T(2,128)(2,1)S(1)}, u32[]{:S(2)}, u32[]{:S(2)}) async-start(bf16[2,2,32768]{2,1,0:T(2,128)(2,1)} %reshape.424), calls=%async_computation.1 | async-start | bytes 524288 | tf_op jit(solution)/shard_map/all_to_all | solution.py:92
  98.6 4.7 %all-to-all-done.1 = bf16[2,2,32768]{2,1,0:T(2,128)(2,1)S(1)} async-done(((bf16[2,2,32768]{2,1,0:T(2,128)(2,1)}), bf16[2,2,32768]{2,1,0:T(2,128)(2,1)S(1)}, u32[]{:S(2)}, u32[]{:S(2)}) %all-to-all-start.1) | async-done | bytes 262176 | tf_op jit(solution)/shard_map/all_to_all | solution.py:92
  103.3 3.6 %all-to-all-start.2 = ((bf16[2,2,32768]{2,1,0:T(2,128)(2,1)}), bf16[2,2,32768]{2,1,0:T(2,128)(2,1)S(1)}, u32[]{:S(2)}, u32[]{:S(2)}) async-start(bf16[2,2,32768]{2,1,0:T(2,128)(2,1)} %reshape.426), calls=%async_computation.2 | async-start | bytes 524288 | tf_op jit(solution)/shard_map/all_to_all | solution.py:93
  107.3 4.6 %all-to-all-done.2 = bf16[2,2,32768]{2,1,0:T(2,128)(2,1)S(1)} async-done(((bf16[2,2,32768]{2,1,0:T(2,128)(2,1)}), bf16[2,2,32768]{2,1,0:T(2,128)(2,1)S(1)}, u32[]{:S(2)}, u32[]{:S(2)}) %all-to-all-start.2) | async-done | bytes 262176 | tf_op jit(solution)/shard_map/all_to_all | solution.py:93
  112.3 0.8 copy_convert_fusion.1
  113.1 1.0 copy.67
  114.4 1.0 copy.60
  115.4 1.2 copy.61
  116.7 2.3 %fusion.6 = f32[1,32,16,2,128]{4,2,3,1,0:T(8,128)S(1)} fusion(bf16[32,128,128]{1,2,0:T(8,128)(2,1)} %get-tuple-element.15, bf16[32,128,128]{1,2,0:T(8,128)(2,1)} %get-tuple-element.14, bf16[1,32,16,2,128]{4,2,1,3,0:T(8,128)(2,1)S(1)} %bitcast.196, bf16[1,32,16,2,128]{4,2,1,3,0:T(8,128)(2,1)S(1)} %bitcast.170), kind=kOutput, calls=%fused_computation.9 | convolution fusion | flops 72351744 | bytes 3145728 | tf_op jit(solution)/shard_map/wgcbs,gst->wgcbt/dot_general | solution.py:62
  120.0 1.9 fusion.7
  122.9 2.3 %fusion.16 = (bf16[1,512,256]{1,2,0:T(8,128)(2,1)}, bf16[1,512,256]{1,2,0:T(8,128)(2,1)S(1)}, bf16[1,512,256]{1,2,0:T(8,128)(2,1)}, bf16[1,512,256]{1,2,0:T(8,128)(2,1)S(1)}) fusion(f32[1,512,2,128]{1,3,2,0:T(8,128)} %copy.60, f32[1,512,256]{1,2,0:T(8,128)S(1)} %copy.74, f32[512]{0:T(512)S(1)} %dynamic_slice.7, f32[1,512,2,128]{1,3,2,0:T(8,128)S(1)} %copy.50, ...), kind=kLoop, calls=%fused_computation.30 | loop fusion | flops 1835008 | bytes 4196352 | tf_op jit(solution)/shard_map/convert_element_type | solution.py:69
  126.0 2.2 %reduce.7 = bf16[256,512]{1,0:T(8,128)(2,1)S(1)} reduce(bf16[256,1,512]{2,1,0:T(2,128)(2,1)S(1)} %bitcast.184, bf16[]{:T(256)} %broadcast.146), dimensions={1}, to_apply=%bitcast.148.reduce_sub_computation | reduce | bytes 524290
  128.2 0.9 reshape.434
  129.1 3.4 %all-to-all-start.6 = ((bf16[2,2,32768]{2,1,0:T(2,128)(2,1)}), bf16[2,2,32768]{2,1,0:T(2,128)(2,1)S(1)}, u32[]{:S(2)}, u32[]{:S(2)}) async-start(bf16[2,2,32768]{2,1,0:T(2,128)(2,1)} %reshape.434), calls=%async_computation.6 | async-start | bytes 524288 | tf_op jit(solution)/shard_map/all_to_all | solution.py:107
  132.6 2.7 %fusion.8 = f32[32,128,256,1]{2,1,0,3:T(8,128)} fusion(bf16[32,16,2,128]{3,1,0,2:T(8,128)(2,1)S(1)} %bitcast.171, bf16[1,32,16,2,128]{4,2,1,3,0:T(8,128)(2,1)S(1)} %bitcast.167, bf16[1,32,16,2,128]{4,2,1,3,0:T(8,128)(2,1)S(1)} %bitcast.191), kind=kOutput, calls=%fused_computation.17 | convolution fusion | flops 68157440 | bytes 4980736 | tf_op jit(solution)/shard_map/wgcbt,wgcbs->gts/dot_general | solution.py:71
  135.7 2.2 %reduce.8 = bf16[256,512]{1,0:T(8,128)(2,1)S(1)} reduce(bf16[256,1,512]{2,1,0:T(2,128)(2,1)S(1)} %bitcast.185, bf16[]{:T(256)} %broadcast.146), dimensions={1}, to_apply=%bitcast.147.reduce_sub_computation | reduce | bytes 524290
  137.9 0.9 reshape.436
  139.2 2.2 %reduce.5 = bf16[256,512]{1,0:T(8,128)(2,1)S(1)} reduce(bf16[256,1,512]{2,1,0:T(2,128)(2,1)S(1)} %bitcast.186, bf16[]{:T(256)} %broadcast.146), dimensions={1}, to_apply=%bitcast.150.reduce_sub_computation | reduce | bytes 524290
  141.4 0.9 reshape.428
  142.7 2.2 %reduce.6 = bf16[256,512]{1,0:T(8,128)(2,1)S(1)} reduce(bf16[256,1,512]{2,1,0:T(2,128)(2,1)S(1)} %bitcast.181, bf16[]{:T(256)} %broadcast.146), dimensions={1}, to_apply=%bitcast.149.reduce_sub_computation | reduce | bytes 524290
  144.9 0.9 reshape.432
  145.8 4.6 %copy.93 = f32[4,8,128,256]{3,1,2,0:T(8,128)S(1)} copy(f32[4,8,128,256]{3,2,1,0:T(8,128)} %bitcast.154) | data formatting | bytes 8388608
  150.4 2.3 %pad.6 = f32[32,32896]{1,0:T(8,128)} pad(f32[32,32768]{1,0:T(8,128)S(1)} %bitcast.155, f32[]{:T(128)} %constant.40.clone.1), padding=0_0x0_128 | pad | bytes 8404996 | tf_op jit(solution)/shard_map/jit(_pad)/pad | solution.py:26
  152.8 8.0 %reshape.397 = f32[32,128,257]{2,1,0:T(8,128)} reshape(f32[32,32896]{1,0:T(8,128)} %pad.6) | data formatting | bytes 8421376 | tf_op jit(solution)/shard_map/reshape | solution.py:27
  160.7 3.3 %reduce_sum.18 = f32[32,257]{1,0:T(8,128)S(1)} reduce(f32[32,128,257]{2,1,0:T(8,128)} %reshape.397, f32[]{:T(128)} %constant.40.clone.1), dimensions={1}, to_apply=%region_0.1 | reduce | flops 1044448 | bytes 4243588 | tf_op jit(solution)/shard_map/reduce_sum | solution.py:28
  164.2 3.4 %all-to-all-start.7 = ((bf16[2,2,32768]{2,1,0:T(2,128)(2,1)}), bf16[2,2,32768]{2,1,0:T(2,128)(2,1)S(1)}, u32[]{:S(2)}, u32[]{:S(2)}) async-start(bf16[2,2,32768]{2,1,0:T(2,128)(2,1)} %reshape.436), calls=%async_computation.7 | async-start | bytes 524288 | tf_op jit(solution)/shard_map/all_to_all | solution.py:108
  167.8 19.4 %all-reduce.3 = (f32[32,128]{1,0:T(8,128)S(1)}, f32[512]{0:T(512)S(1)}) all-reduce(f32[32,128]{1,0:T(8,128)S(1)} %rev.3, f32[512]{0:T(512)S(1)} %multiply_reduce_fusion), channel_id=1, replica_groups=mesh['ctx'=2,'dp'=4,'tp'=4] {'dp'}, use_global_device_ids=true, to_apply=%region_1.2 | all-reduce | flops 4608 | bytes 36864 | tf_op jit(solution)/shard_map/psum | solution.py:110
  187.2 4.3 %all-gather = f32[2,1,512]{2,1,0:T(1,128)S(1)} all-gather(f32[1,1,512]{2,1,0:T(1,128)S(1)} %bitcast.202), channel_id=1, replica_groups=mesh['ctx'=2,'dp'=4,'tp'=4] {'ctx'}, dimensions={0}, use_global_device_ids=true | all-gather | bytes 6144 | tf_op jit(solution)/shard_map/all_gather | solution.py:113
  191.6 4.4 %all_gather.6 = f32[64,128]{1,0:T(8,128)S(1)} all-gather(f32[32,128]{1,0:T(8,128)S(1)} %get-tuple-element.6), channel_id=1, replica_groups=mesh['ctx'=2,'dp'=4,'tp'=4] {'ctx'}, dimensions={0}, use_global_device_ids=true | all-gather | bytes 49152 | tf_op jit(solution)/shard_map/all_gather | solution.py:112
  196.0 3.4 %all-to-all-start.3 = ((bf16[2,2,32768]{2,1,0:T(2,128)(2,1)}), bf16[2,2,32768]{2,1,0:T(2,128)(2,1)S(1)}, u32[]{:S(2)}, u32[]{:S(2)}) async-start(bf16[2,2,32768]{2,1,0:T(2,128)(2,1)} %reshape.428), calls=%async_computation.3 | async-start | bytes 524288 | tf_op jit(solution)/shard_map/all_to_all | solution.py:105
  200.0 4.6 %all-to-all-done.3 = bf16[2,2,32768]{2,1,0:T(2,128)(2,1)S(1)} async-done(((bf16[2,2,32768]{2,1,0:T(2,128)(2,1)}), bf16[2,2,32768]{2,1,0:T(2,128)(2,1)S(1)}, u32[]{:S(2)}, u32[]{:S(2)}) %all-to-all-start.3) | async-done | bytes 262176 | tf_op jit(solution)/shard_map/all_to_all | solution.py:105
  204.6 3.4 %all-to-all-start.5 = ((bf16[2,2,32768]{2,1,0:T(2,128)(2,1)}), bf16[2,2,32768]{2,1,0:T(2,128)(2,1)S(1)}, u32[]{:S(2)}, u32[]{:S(2)}) async-start(bf16[2,2,32768]{2,1,0:T(2,128)(2,1)} %reshape.432), calls=%async_computation.5 | async-start | bytes 524288 | tf_op jit(solution)/shard_map/all_to_all | solution.py:106
  209.0 0.8 copy.76
  210.1 0.8 copy.78
  211.3 0.8 copy.64
  212.1 1.1 all-to-all-done.5
  (69 shorter events, 14.8 us)
Async XLA Ops:
  0.6 10.0 %copy-start = (f32[64,128]{1,0:T(8,128)S(1)}, f32[64,128]{1,0:T(8,128)}, u32[]{:S(2)}) copy-start(f32[64,128]{1,0:T(8,128)} %param.12) | copy-start | bytes 98308
  6.3 79.1 %all-to-all-start.4 = ((bf16[2,2,32768]{2,1,0:T(2,128)(2,1)}), bf16[2,2,32768]{2,1,0:T(2,128)(2,1)S(1)}, u32[]{:S(2)}, u32[]{:S(2)}) async-start(bf16[2,2,32768]{2,1,0:T(2,128)(2,1)} %reshape.430), calls=%async_computation.4 | async-start | bytes 524288 | tf_op jit(solution)/shard_map/all_to_all | solution.py:94
  72.2 3.0 %copy-start.3 = (bf16[1,1024,128]{2,1,0:T(8,128)(2,1)S(1)}, bf16[1,1024,128]{2,1,0:T(8,128)(2,1)}, u32[]{:S(2)}) copy-start(bf16[1,1024,128]{2,1,0:T(8,128)(2,1)} %param.7) | copy-start | bytes 786436
  72.2 6.3 %copy-start.4 = (bf16[1,1024,128]{2,1,0:T(8,128)(2,1)S(1)}, bf16[1,1024,128]{2,1,0:T(8,128)(2,1)}, u32[]{:S(2)}) copy-start(bf16[1,1024,128]{2,1,0:T(8,128)(2,1)} %param.8) | copy-start | bytes 786436
  73.7 8.2 %copy-start.5 = (bf16[1,1024,128]{2,1,0:T(8,128)(2,1)S(1)}, bf16[1,1024,128]{2,1,0:T(8,128)(2,1)}, u32[]{:S(2)}) copy-start(bf16[1,1024,128]{2,1,0:T(8,128)(2,1)} %param.9) | copy-start | bytes 786436
  73.7 11.6 %copy-start.6 = (f32[1024]{0:T(1024)S(1)}, f32[1024]{0:T(1024)}, u32[]{:S(2)}) copy-start(f32[1024]{0:T(1024)} %param.13) | copy-start | bytes 12292
  85.4 9.3 %all-to-all-start = ((bf16[2,2,32768]{2,1,0:T(2,128)(2,1)}), bf16[2,2,32768]{2,1,0:T(2,128)(2,1)S(1)}, u32[]{:S(2)}, u32[]{:S(2)}) async-start(bf16[2,2,32768]{2,1,0:T(2,128)(2,1)} %reshape.422), calls=%async_computation | async-start | bytes 524288 | tf_op jit(solution)/shard_map/all_to_all | solution.py:91
  94.7 8.6 %all-to-all-start.1 = ((bf16[2,2,32768]{2,1,0:T(2,128)(2,1)}), bf16[2,2,32768]{2,1,0:T(2,128)(2,1)S(1)}, u32[]{:S(2)}, u32[]{:S(2)}) async-start(bf16[2,2,32768]{2,1,0:T(2,128)(2,1)} %reshape.424), calls=%async_computation.1 | async-start | bytes 524288 | tf_op jit(solution)/shard_map/all_to_all | solution.py:92
  103.3 8.6 %all-to-all-start.2 = ((bf16[2,2,32768]{2,1,0:T(2,128)(2,1)}), bf16[2,2,32768]{2,1,0:T(2,128)(2,1)S(1)}, u32[]{:S(2)}, u32[]{:S(2)}) async-start(bf16[2,2,32768]{2,1,0:T(2,128)(2,1)} %reshape.426), calls=%async_computation.2 | async-start | bytes 524288 | tf_op jit(solution)/shard_map/all_to_all | solution.py:93
  125.6 9.7 %copy-start.2 = (bf16[1,512,256]{1,2,0:T(8,128)(2,1)S(1)}, bf16[1,512,256]{1,2,0:T(8,128)(2,1)}, u32[]{:S(2)}) copy-start(bf16[1,512,256]{1,2,0:T(8,128)(2,1)} %get-tuple-element.8) | copy-start | bytes 786436
  129.1 35.1 %all-to-all-start.6 = ((bf16[2,2,32768]{2,1,0:T(2,128)(2,1)}), bf16[2,2,32768]{2,1,0:T(2,128)(2,1)S(1)}, u32[]{:S(2)}, u32[]{:S(2)}) async-start(bf16[2,2,32768]{2,1,0:T(2,128)(2,1)} %reshape.434), calls=%async_computation.6 | async-start | bytes 524288 | tf_op jit(solution)/shard_map/all_to_all | solution.py:107
  132.6 9.8 %copy-start.1 = (bf16[1,512,256]{1,2,0:T(8,128)(2,1)S(1)}, bf16[1,512,256]{1,2,0:T(8,128)(2,1)}, u32[]{:S(2)}) copy-start(bf16[1,512,256]{1,2,0:T(8,128)(2,1)} %get-tuple-element.12) | copy-start | bytes 786436
  164.2 31.8 %all-to-all-start.7 = ((bf16[2,2,32768]{2,1,0:T(2,128)(2,1)}), bf16[2,2,32768]{2,1,0:T(2,128)(2,1)S(1)}, u32[]{:S(2)}, u32[]{:S(2)}) async-start(bf16[2,2,32768]{2,1,0:T(2,128)(2,1)} %reshape.436), calls=%async_computation.7 | async-start | bytes 524288 | tf_op jit(solution)/shard_map/all_to_all | solution.py:108
  196.0 8.6 %all-to-all-start.3 = ((bf16[2,2,32768]{2,1,0:T(2,128)(2,1)}), bf16[2,2,32768]{2,1,0:T(2,128)(2,1)S(1)}, u32[]{:S(2)}, u32[]{:S(2)}) async-start(bf16[2,2,32768]{2,1,0:T(2,128)(2,1)} %reshape.428), calls=%async_computation.3 | async-start | bytes 524288 | tf_op jit(solution)/shard_map/all_to_all | solution.py:105
  204.6 8.6 %all-to-all-start.5 = ((bf16[2,2,32768]{2,1,0:T(2,128)(2,1)}), bf16[2,2,32768]{2,1,0:T(2,128)(2,1)S(1)}, u32[]{:S(2)}, u32[]{:S(2)}) async-start(bf16[2,2,32768]{2,1,0:T(2,128)(2,1)} %reshape.432), calls=%async_computation.5 | async-start | bytes 524288 | tf_op jit(solution)/shard_map/all_to_all | solution.py:106
where the time goes:
time: 215 us; the launch traced here: 214 us
  local copies, waits for them, and re-layouts  97.8 us (45%)
  other arithmetic  31.3 us (15%)
  starting transfers between devices  28.5 us (13%)
  blocking collectives  28.2 us (13%)
  waiting for transfers between devices  20.6 us (10%)
  matrix products  6.98 us (3%)
    gather x2, local copies, waits for them, and re-layouts, tap_matrices(): spread = tap_rows[:, jnp.mod(target - source, tap_len)]  61.4 us
    psum x1, blocking collectives, body(): replica = lax.psum((results[4], results[5]), 'dp')  19.4 us
    unnamed x9, other arithmetic  19.2 us
    unnamed x40, local copies, waits for them, and re-layouts  15.5 us
    reshape x1, local copies, waits for them, and re-layouts, diagonal_sums(): skewed = flattened.reshape(groups, tap_len, double_len + 1)  7.98 us
    all_to_all x1, waiting for transfers between devices, body(): lax.all_to_all(query_act, 'ctx', split_axis=1, concat_axis=2, tiled=True)  5.54 us
    all_to_all x1, waiting for transfers between devices, body(): lax.all_to_all(key_act, 'ctx', split_axis=1, concat_axis=2, tiled=True)  4.75 us
    all_to_all x1, waiting for transfers between devices, body(): lax.all_to_all(value_act, 'ctx', split_axis=1, concat_axis=2, tiled=True)  4.65 us
  transfers between devices with their start and end apart: 8, of which 5 were waited for; matrix products, arithmetic and copies ran while one was open for 52% of the time, Pallas kernels for 0%

commit v1 on v0

--- a/solution.py
+++ b/solution.py
@@ -89,7 +89,12 @@
     scaled_grad = out_grad * keep_mask.astype(jnp.bfloat16)[:, None, :]
     moved = (
         lax.all_to_all(query_act, "ctx", split_axis=1, concat_axis=2, tiled=True),
-        lax.all_to_all(key_act, "ctx", split_axis=1, concat_axis=2, tiled=True),
+        jnp.concatenate(
+            lax.all_to_all(
+                jnp.stack(jnp.split(key_act, lax.axis_size("ctx"), axis=1)), "ctx", 0, 0
+            ),
+            axis=2,
+        ),
         lax.all_to_all(value_act, "ctx", split_axis=1, concat_axis=2, tiled=True),
         lax.all_to_all(scaled_grad, "ctx", split_axis=1, concat_axis=2, tiled=True),
     )

time: 215 us -> 212 us (0.986)
  local copies, waits for them, and re-layouts: 97.8 us -> 94.8 us
    unnamed x9 -> x8, other arithmetic: 19.2 us -> 17 us
    unnamed x40 -> x45, local copies, waits for them, and re-layouts: 15.5 us -> 14 us
  transfers between devices with their start and end apart: 8 -> 8, of which waited for: 5 -> 6; matrix products, arithmetic and copies ran while one was open for 52% -> 53% of each run, Pallas kernels for 0% -> 0%
where the time goes in v1:
time: 212 us; the launch traced here: 210 us
  local copies, waits for them, and re-layouts  94.8 us (45%)
  other arithmetic  29.2 us (14%)
  starting transfers between devices  28.7 us (14%)
  blocking collectives  28.3 us (13%)
  waiting for transfers between devices  21 us (10%)
  matrix products  7.09 us (3%)
    gather x2, local copies, waits for them, and re-layouts, tap_matrices(): spread = tap_rows[:, jnp.mod(target - source, tap_len)]  61.8 us
    psum x1, blocking collectives, body(): replica = lax.psum((results[4], results[5]), 'dp')  19.6 us
    unnamed x8, other arithmetic  17 us
    unnamed x45, local copies, waits for them, and re-layouts  14 us
    reshape x1, local copies, waits for them, and re-layouts, diagonal_sums(): skewed = flattened.reshape(groups, tap_len, double_len + 1)  7.96 us
    all_to_all x1, waiting for transfers between devices, body(): lax.all_to_all(jnp.stack(jnp.split(key_act, lax.axis_size('ctx'), axis=1)...  5.34 us
    all_to_all x1, waiting for transfers between devices, body(): lax.all_to_all(results[0], 'ctx', split_axis=2, concat_axis=1, tiled=True)  4.54 us
    all_gather x1, blocking collectives, body(): lax.all_gather(replica[0], 'ctx', axis=0, tiled=True)  4.4 us
  transfers between devices with their start and end apart: 8, of which 6 were waited for; matrix products, arithmetic and copies ran while one was open for 53% of the time, Pallas kernels for 0%

profile of v1, /device:TPU:0, one launch (start us, length us, event | category | flops | bytes accessed | tf_op | source)
XLA Modules:
  0.0 210.4 jit_solution(15993957530461640886)
XLA Ops:
  1.3 1.5 fusion.30
  3.3 2.2 %reduce.3 = bf16[1024,128]{1,0:T(8,128)(2,1)S(1)} reduce(bf16[1024,1,128]{2,1,0:T(2,128)(2,1)S(1)} %fusion.30, bf16[]{:T(256)} %broadcast.146), dimensions={1}, to_apply=%fusion.30.reduce_sub_computation | reduce | bytes 524290
  6.3 4.2 %all-to-all-start.4 = ((bf16[2,2,32768]{2,1,0:T(2,128)(2,1)}), bf16[2,2,32768]{2,1,0:T(2,128)(2,1)S(1)}, u32[]{:S(2)}, u32[]{:S(2)}) async-start(bf16[2,2,32768]{2,1,0:T(2,128)(2,1)} %reshape.426), calls=%async_computation.4 | async-start | bytes 524288 | tf_op jit(solution)/shard_map/all_to_all | solution.py:99
  10.8 57.8 %gather_fusion = bf16[16384,32]{1,0:T(8,128)(2,1)} fusion(bf16[32,128]{0,1:T(8,128)(2,1)S(1)} %copy.95, s32[16384]{0:T(1024)S(1)} %fusion.22), kind=kCustom, calls=%fused_computation | custom fusion | bytes 2162688 | tf_op jit(solution)/shard_map/gather | solution.py:12
  68.6 4.0 %copy.85 = bf16[128,128,32]{1,0,2:T(8,128)(2,1)S(1)} copy(bf16[128,128,32]{2,1,0:T(8,128)(2,1)} %bitcast.160) | data formatting | bytes 2097152 | tf_op jit(solution)/shard_map/gather | solution.py:12
  72.6 1.5 bitcast_select_fusion.1
  74.1 1.5 select_bitcast_fusion.1
  76.0 2.2 %reduce.2 = bf16[1024,128]{1,0:T(8,128)(2,1)S(1)} reduce(bf16[1024,1,128]{2,1,0:T(2,128)(2,1)S(1)} %bitcast.181, bf16[]{:T(256)} %broadcast.146), dimensions={1}, to_apply=%bitcast.157.reduce_sub_computation | reduce | bytes 524290
  78.2 0.8 reshape.420
  79.4 2.2 %reduce.1 = bf16[1024,128]{1,0:T(8,128)(2,1)S(1)} reduce(bf16[1024,1,128]{2,1,0:T(2,128)(2,1)S(1)} %bitcast.182, bf16[]{:T(256)} %broadcast.146), dimensions={1}, to_apply=%bitcast.156.reduce_sub_computation | reduce | bytes 524290
  81.6 0.8 reshape.422
  83.2 3.5 %all-to-all-start.1 = ((bf16[2,1,512,128]{3,2,1,0:T(8,128)(2,1)}), bf16[2,1,512,128]{3,2,1,0:T(8,128)(2,1)S(1)}, u32[]{:S(2)}, u32[]{:S(2)}) async-start(bf16[2,1,512,128]{3,2,1,0:T(8,128)(2,1)} %pad_maximum_fusion.2), calls=%async_computation.1 | async-start | bytes 524288 | tf_op jit(solution)/shard_map/all_to_all | solution.py:93
  87.2 5.3 %all-to-all-done.1 = bf16[2,1,512,128]{3,2,1,0:T(8,128)(2,1)S(1)} async-done(((bf16[2,1,512,128]{3,2,1,0:T(8,128)(2,1)}), bf16[2,1,512,128]{3,2,1,0:T(8,128)(2,1)S(1)}, u32[]{:S(2)}, u32[]{:S(2)}) %all-to-all-start.1) | async-done | bytes 262176 | tf_op jit(solution)/shard_map/all_to_all | solution.py:93
  92.5 3.4 %all-to-all-start = ((bf16[2,2,32768]{2,1,0:T(2,128)(2,1)}), bf16[2,2,32768]{2,1,0:T(2,128)(2,1)S(1)}, u32[]{:S(2)}, u32[]{:S(2)}) async-start(bf16[2,2,32768]{2,1,0:T(2,128)(2,1)} %reshape.420), calls=%async_computation | async-start | bytes 524288 | tf_op jit(solution)/shard_map/all_to_all | solution.py:91
  96.0 1.0 copy.63
  97.1 4.1 %all-to-all-done = bf16[2,2,32768]{2,1,0:T(2,128)(2,1)S(1)} async-done(((bf16[2,2,32768]{2,1,0:T(2,128)(2,1)}), bf16[2,2,32768]{2,1,0:T(2,128)(2,1)S(1)}, u32[]{:S(2)}, u32[]{:S(2)}) %all-to-all-start) | async-done | bytes 262176 | tf_op jit(solution)/shard_map/all_to_all | solution.py:91
  101.2 3.6 %all-to-all-start.2 = ((bf16[2,2,32768]{2,1,0:T(2,128)(2,1)}), bf16[2,2,32768]{2,1,0:T(2,128)(2,1)S(1)}, u32[]{:S(2)}, u32[]{:S(2)}) async-start(bf16[2,2,32768]{2,1,0:T(2,128)(2,1)} %reshape.422), calls=%async_computation.2 | async-start | bytes 524288 | tf_op jit(solution)/shard_map/all_to_all | solution.py:98
  105.4 4.3 %all-to-all-done.2 = bf16[2,2,32768]{2,1,0:T(2,128)(2,1)S(1)} async-done(((bf16[2,2,32768]{2,1,0:T(2,128)(2,1)}), bf16[2,2,32768]{2,1,0:T(2,128)(2,1)S(1)}, u32[]{:S(2)}, u32[]{:S(2)}) %all-to-all-start.2) | async-done | bytes 262176 | tf_op jit(solution)/shard_map/all_to_all | solution.py:98
  111.1 2.4 %fusion.6 = f32[1,32,16,2,128]{4,2,3,1,0:T(8,128)S(1)} fusion(bf16[32,128,128]{1,2,0:T(8,128)(2,1)} %get-tuple-element.17, bf16[32,128,128]{1,2,0:T(8,128)(2,1)} %get-tuple-element.16, bf16[1,32,16,2,128]{4,2,1,3,0:T(8,128)(2,1)S(1)} %bitcast.193, bf16[1,32,16,2,128]{4,2,1,3,0:T(8,128)(2,1)S(1)} %bitcast.169), kind=kOutput, calls=%fused_computation.9 | convolution fusion | flops 72351744 | bytes 3145728 | tf_op jit(solution)/shard_map/wgcbs,gst->wgcbt/dot_general | solution.py:62
  114.5 1.9 fusion.7
  117.4 2.1 fusion.16
  120.3 2.2 %reduce.6 = bf16[256,512]{1,0:T(8,128)(2,1)S(1)} reduce(bf16[256,1,512]{2,1,0:T(2,128)(2,1)S(1)} %bitcast.178, bf16[]{:T(256)} %broadcast.146), dimensions={1}, to_apply=%bitcast.153.reduce_sub_computation | reduce | bytes 524290
  122.5 0.9 reshape.430
  123.4 3.4 %all-to-all-start.6 = ((bf16[2,2,32768]{2,1,0:T(2,128)(2,1)}), bf16[2,2,32768]{2,1,0:T(2,128)(2,1)S(1)}, u32[]{:S(2)}, u32[]{:S(2)}) async-start(bf16[2,2,32768]{2,1,0:T(2,128)(2,1)} %reshape.430), calls=%async_computation.6 | async-start | bytes 524288 | tf_op jit(solution)/shard_map/all_to_all | solution.py:112
  127.3 2.2 %reduce.7 = bf16[256,512]{1,0:T(8,128)(2,1)S(1)} reduce(bf16[256,1,512]{2,1,0:T(2,128)(2,1)S(1)} %bitcast.179, bf16[]{:T(256)} %broadcast.146), dimensions={1}, to_apply=%bitcast.152.reduce_sub_computation | reduce | bytes 524290
  129.5 0.9 reshape.432
  130.4 1.6 all-to-all-done.6
  132.0 3.7 %all-to-all-start.7 = ((bf16[2,2,32768]{2,1,0:T(2,128)(2,1)}), bf16[2,2,32768]{2,1,0:T(2,128)(2,1)S(1)}, u32[]{:S(2)}, u32[]{:S(2)}) async-start(bf16[2,2,32768]{2,1,0:T(2,128)(2,1)} %reshape.432), calls=%async_computation.7 | async-start | bytes 524288 | tf_op jit(solution)/shard_map/all_to_all | solution.py:113
  135.7 2.7 %fusion.8 = f32[32,128,256,1]{2,1,0,3:T(8,128)} fusion(bf16[32,16,2,128]{3,1,0,2:T(8,128)(2,1)S(1)} %bitcast.170, bf16[1,32,16,2,128]{4,2,1,3,0:T(8,128)(2,1)S(1)} %bitcast.186, bf16[1,32,16,2,128]{4,2,1,3,0:T(8,128)(2,1)S(1)} %bitcast.188), kind=kOutput, calls=%fused_computation.17 | convolution fusion | flops 68157440 | bytes 4980736 | tf_op jit(solution)/shard_map/wgcbt,wgcbs->gts/dot_general | solution.py:71
  138.8 2.2 %reduce.4 = bf16[256,512]{1,0:T(8,128)(2,1)S(1)} reduce(bf16[256,1,512]{2,1,0:T(2,128)(2,1)S(1)} %bitcast.180, bf16[]{:T(256)} %broadcast.146), dimensions={1}, to_apply=%bitcast.155.reduce_sub_computation | reduce | bytes 524290
  141.0 0.9 reshape.424
  142.3 2.2 %reduce.5 = bf16[256,512]{1,0:T(8,128)(2,1)S(1)} reduce(bf16[256,1,512]{2,1,0:T(2,128)(2,1)S(1)} %bitcast.175, bf16[]{:T(256)} %broadcast.146), dimensions={1}, to_apply=%bitcast.154.reduce_sub_computation | reduce | bytes 524290
  144.5 0.9 reshape.428
  145.4 4.6 %copy.96 = f32[4,8,128,256]{3,1,2,0:T(8,128)S(1)} copy(f32[4,8,128,256]{3,2,1,0:T(8,128)} %bitcast.158) | data formatting | bytes 8388608
  150.0 2.3 %pad.6 = f32[32,32896]{1,0:T(8,128)} pad(f32[32,32768]{1,0:T(8,128)S(1)} %bitcast.159, f32[]{:T(128)} %constant.40.clone.1), padding=0_0x0_128 | pad | bytes 8404996 | tf_op jit(solution)/shard_map/jit(_pad)/pad | solution.py:26
  152.3 8.0 %reshape.395 = f32[32,128,257]{2,1,0:T(8,128)} reshape(f32[32,32896]{1,0:T(8,128)} %pad.6) | data formatting | bytes 8421376 | tf_op jit(solution)/shard_map/reshape | solution.py:27
  160.3 3.3 %reduce_sum.18 = f32[32,257]{1,0:T(8,128)S(1)} reduce(f32[32,128,257]{2,1,0:T(8,128)} %reshape.395, f32[]{:T(128)} %constant.40.clone.1), dimensions={1}, to_apply=%region_0.1 | reduce | flops 1044448 | bytes 4243588 | tf_op jit(solution)/shard_map/reduce_sum | solution.py:28
  163.7 19.6 %all-reduce.3 = (f32[32,128]{1,0:T(8,128)S(1)}, f32[512]{0:T(512)S(1)}) all-reduce(f32[32,128]{1,0:T(8,128)S(1)} %rev.3, f32[512]{0:T(512)S(1)} %get-tuple-element.8), channel_id=1, replica_groups=mesh['ctx'=2,'dp'=4,'tp'=4] {'dp'}, use_global_device_ids=true, to_apply=%region_1.2 | all-reduce | flops 4608 | bytes 36864 | tf_op jit(solution)/shard_map/psum | solution.py:115
  183.3 4.3 %all-gather = f32[2,1,512]{2,1,0:T(1,128)S(1)} all-gather(f32[1,1,512]{2,1,0:T(1,128)S(1)} %bitcast.199), channel_id=1, replica_groups=mesh['ctx'=2,'dp'=4,'tp'=4] {'ctx'}, dimensions={0}, use_global_device_ids=true | all-gather | bytes 6144 | tf_op jit(solution)/shard_map/all_gather | solution.py:118
  187.6 4.4 %all_gather.6 = f32[64,128]{1,0:T(8,128)S(1)} all-gather(f32[32,128]{1,0:T(8,128)S(1)} %get-tuple-element.6), channel_id=1, replica_groups=mesh['ctx'=2,'dp'=4,'tp'=4] {'ctx'}, dimensions={0}, use_global_device_ids=true | all-gather | bytes 49152 | tf_op jit(solution)/shard_map/all_gather | solution.py:117
  192.0 3.4 %all-to-all-start.3 = ((bf16[2,2,32768]{2,1,0:T(2,128)(2,1)}), bf16[2,2,32768]{2,1,0:T(2,128)(2,1)S(1)}, u32[]{:S(2)}, u32[]{:S(2)}) async-start(bf16[2,2,32768]{2,1,0:T(2,128)(2,1)} %reshape.424), calls=%async_computation.3 | async-start | bytes 524288 | tf_op jit(solution)/shard_map/all_to_all | solution.py:110
  196.1 4.5 %all-to-all-done.3 = bf16[2,2,32768]{2,1,0:T(2,128)(2,1)S(1)} async-done(((bf16[2,2,32768]{2,1,0:T(2,128)(2,1)}), bf16[2,2,32768]{2,1,0:T(2,128)(2,1)S(1)}, u32[]{:S(2)}, u32[]{:S(2)}) %all-to-all-start.3) | async-done | bytes 262176 | tf_op jit(solution)/shard_map/all_to_all | solution.py:110
  200.7 3.4 %all-to-all-start.5 = ((bf16[2,2,32768]{2,1,0:T(2,128)(2,1)}), bf16[2,2,32768]{2,1,0:T(2,128)(2,1)S(1)}, u32[]{:S(2)}, u32[]{:S(2)}) async-start(bf16[2,2,32768]{2,1,0:T(2,128)(2,1)} %reshape.428), calls=%async_computation.5 | async-start | bytes 524288 | tf_op jit(solution)/shard_map/all_to_all | solution.py:111
  205.0 0.8 copy.79
  206.2 0.8 copy.81
  207.3 0.8 copy.67
  208.2 1.1 all-to-all-done.5
  209.6 0.8 copy.72
  (74 shorter events, 12.7 us)
Async XLA Ops:
  0.6 10.0 %copy-start = (f32[64,128]{1,0:T(8,128)S(1)}, f32[64,128]{1,0:T(8,128)}, u32[]{:S(2)}) copy-start(f32[64,128]{1,0:T(8,128)} %param.12) | copy-start | bytes 98308
  6.3 76.9 %all-to-all-start.4 = ((bf16[2,2,32768]{2,1,0:T(2,128)(2,1)}), bf16[2,2,32768]{2,1,0:T(2,128)(2,1)S(1)}, u32[]{:S(2)}, u32[]{:S(2)}) async-start(bf16[2,2,32768]{2,1,0:T(2,128)(2,1)} %reshape.426), calls=%async_computation.4 | async-start | bytes 524288 | tf_op jit(solution)/shard_map/all_to_all | solution.py:99
  72.6 3.0 %copy-start.9 = (bf16[1,1024,128]{2,1,0:T(8,128)(2,1)S(1)}, bf16[1,1024,128]{2,1,0:T(8,128)(2,1)}, u32[]{:S(2)}) copy-start(bf16[1,1024,128]{2,1,0:T(8,128)(2,1)} %param.8) | copy-start | bytes 786436
  72.6 3.0 %copy-start.7 = (bf16[1,1024,128]{2,1,0:T(8,128)(2,1)S(1)}, bf16[1,1024,128]{2,1,0:T(8,128)(2,1)}, u32[]{:S(2)}) copy-start(bf16[1,1024,128]{2,1,0:T(8,128)(2,1)} %param.7) | copy-start | bytes 786436
  72.6 6.4 %copy-start.8 = (bf16[1,1024,128]{2,1,0:T(8,128)(2,1)S(1)}, bf16[1,1024,128]{2,1,0:T(8,128)(2,1)}, u32[]{:S(2)}) copy-start(bf16[1,1024,128]{2,1,0:T(8,128)(2,1)} %param.9) | copy-start | bytes 786436
  74.1 8.3 %copy-start.10 = (f32[1024]{0:T(1024)S(1)}, f32[1024]{0:T(1024)}, u32[]{:S(2)}) copy-start(f32[1024]{0:T(1024)} %param.13) | copy-start | bytes 12292
  83.2 9.3 %all-to-all-start.1 = ((bf16[2,1,512,128]{3,2,1,0:T(8,128)(2,1)}), bf16[2,1,512,128]{3,2,1,0:T(8,128)(2,1)S(1)}, u32[]{:S(2)}, u32[]{:S(2)}) async-start(bf16[2,1,512,128]{3,2,1,0:T(8,128)(2,1)} %pad_maximum_fusion.2), calls=%async_computation.1 | async-start | bytes 524288 | tf_op jit(solution)/shard_map/all_to_all | solution.py:93
  92.5 8.6 %all-to-all-start = ((bf16[2,2,32768]{2,1,0:T(2,128)(2,1)}), bf16[2,2,32768]{2,1,0:T(2,128)(2,1)S(1)}, u32[]{:S(2)}, u32[]{:S(2)}) async-start(bf16[2,2,32768]{2,1,0:T(2,128)(2,1)} %reshape.420), calls=%async_computation | async-start | bytes 524288 | tf_op jit(solution)/shard_map/all_to_all | solution.py:91
  101.2 8.6 %all-to-all-start.2 = ((bf16[2,2,32768]{2,1,0:T(2,128)(2,1)}), bf16[2,2,32768]{2,1,0:T(2,128)(2,1)S(1)}, u32[]{:S(2)}, u32[]{:S(2)}) async-start(bf16[2,2,32768]{2,1,0:T(2,128)(2,1)} %reshape.422), calls=%async_computation.2 | async-start | bytes 524288 | tf_op jit(solution)/shard_map/all_to_all | solution.py:98
  111.0 3.5 %copy-start.1 = (bf16[1,512,2,128]{3,1,2,0:T(8,128)(2,1)}, bf16[1,512,2,128]{3,1,2,0:T(8,128)(2,1)S(1)}, u32[]{:S(2)}) copy-start(bf16[1,512,2,128]{3,1,2,0:T(8,128)(2,1)S(1)} %get-tuple-element.9) | copy-start | bytes 786436
  111.1 3.4 %copy-start.3 = (bf16[1,512,2,128]{3,1,2,0:T(8,128)(2,1)}, bf16[1,512,2,128]{3,1,2,0:T(8,128)(2,1)S(1)}, u32[]{:S(2)}) copy-start(bf16[1,512,2,128]{3,1,2,0:T(8,128)(2,1)S(1)} %concatenate.29) | copy-start | bytes 786436
  119.5 7.3 %copy-start.6 = (bf16[1,512,256]{1,2,0:T(8,128)(2,1)S(1)}, bf16[1,512,256]{1,2,0:T(8,128)(2,1)}, u32[]{:S(2)}) copy-start(bf16[1,512,256]{1,2,0:T(8,128)(2,1)} %get-tuple-element.10) | copy-start | bytes 786436
  119.5 16.1 %copy-start.2 = (bf16[1,512,2,128]{3,1,2,0:T(8,128)(2,1)S(1)}, bf16[1,512,2,128]{3,1,2,0:T(8,128)(2,1)}, u32[]{:S(2)}) copy-start(bf16[1,512,2,128]{3,1,2,0:T(8,128)(2,1)} %copy-done.1) | copy-start | bytes 786436
  119.5 16.1 %copy-start.4 = (bf16[1,512,2,128]{3,1,2,0:T(8,128)(2,1)S(1)}, bf16[1,512,2,128]{3,1,2,0:T(8,128)(2,1)}, u32[]{:S(2)}) copy-start(bf16[1,512,2,128]{3,1,2,0:T(8,128)(2,1)} %copy-done.3) | copy-start | bytes 786436
  123.4 8.6 %all-to-all-start.6 = ((bf16[2,2,32768]{2,1,0:T(2,128)(2,1)}), bf16[2,2,32768]{2,1,0:T(2,128)(2,1)S(1)}, u32[]{:S(2)}, u32[]{:S(2)}) async-start(bf16[2,2,32768]{2,1,0:T(2,128)(2,1)} %reshape.430), calls=%async_computation.6 | async-start | bytes 524288 | tf_op jit(solution)/shard_map/all_to_all | solution.py:112
  129.5 12.4 %copy-start.5 = (bf16[1,512,256]{1,2,0:T(8,128)(2,1)S(1)}, bf16[1,512,256]{1,2,0:T(8,128)(2,1)}, u32[]{:S(2)}) copy-start(bf16[1,512,256]{1,2,0:T(8,128)(2,1)} %get-tuple-element.14) | copy-start | bytes 786436
  132.0 60.0 %all-to-all-start.7 = ((bf16[2,2,32768]{2,1,0:T(2,128)(2,1)}), bf16[2,2,32768]{2,1,0:T(2,128)(2,1)S(1)}, u32[]{:S(2)}, u32[]{:S(2)}) async-start(bf16[2,2,32768]{2,1,0:T(2,128)(2,1)} %reshape.432), calls=%async_computation.7 | async-start | bytes 524288 | tf_op jit(solution)/shard_map/all_to_all | solution.py:113
  192.0 8.6 %all-to-all-start.3 = ((bf16[2,2,32768]{2,1,0:T(2,128)(2,1)}), bf16[2,2,32768]{2,1,0:T(2,128)(2,1)S(1)}, u32[]{:S(2)}, u32[]{:S(2)}) async-start(bf16[2,2,32768]{2,1,0:T(2,128)(2,1)} %reshape.424), calls=%async_computation.3 | async-start | bytes 524288 | tf_op jit(solution)/shard_map/all_to_all | solution.py:110
  200.7 8.6 %all-to-all-start.5 = ((bf16[2,2,32768]{2,1,0:T(2,128)(2,1)}), bf16[2,2,32768]{2,1,0:T(2,128)(2,1)S(1)}, u32[]{:S(2)}, u32[]{:S(2)}) async-start(bf16[2,2,32768]{2,1,0:T(2,128)(2,1)} %reshape.428), calls=%async_computation.5 | async-start | bytes 524288 | tf_op jit(solution)/shard_map/all_to_all | solution.py:111
